TPU v7x, 32 devices: a whole 2x2x4 slice. The times are simulated.
32 devices in a mesh: row: 4 (over z), col: 8 (over y, x, core).
Axes of the slice: x: 2, y: 2, z: 4, core: 2. Of those that a mesh axis runs over, the one named last changes fastest.
Arguments:
- amplitudes: bfloat16 [16, 16, 12, 4096], P('row', 'col'), may hold values from -6 to 6
- integrals: bfloat16 [16, 16, 47, 4096], P('row', 'col'), may hold values from -0.1875 to 0.1875
- pair_lists: int32 [4, 12, 2], replicated, may hold values from 0 to 46, as said below
- tile_counts: int32 [4], replicated, may hold values from 1 to 12, as said below
Outputs:
- symmetric: float32 [16, 16, 12, 4096], P('row', 'col')
Inputs may be any that keep to these rules, and one draw needn't show every extreme that they name: `pair_lists`: each grid row lists 12 distinct ordered pairs of different tiles. `tile_counts`: the largest count equals 12.
All inputs are finite; a program needn't handle non-finite values.
Results may differ from a plain program's by a relative error of at most 0.0029.
Values may be sent and summed in bfloat16 or wider, within the bound.
No kernel may reach another device: no remote copies, remote signals or barrier semaphores. Data moves between devices by JAX's collectives and lax.ppermute only.
A program may use at most 128 MiB of HBM per device.

v0:
```python
import jax
import jax.numpy as jnp
from jax import lax
from jax.sharding import PartitionSpec as P

TILE = 64


def on_device(amplitudes, integrals, pair_lists, tile_counts):
    occ_row, occ_col, slot_count, square = amplitudes.shape
    tile_width = TILE
    row_devices = lax.axis_size("row")
    col_devices = lax.axis_size("col")
    col_ratio = col_devices // row_devices
    my_row = lax.axis_index("row")
    my_col = lax.axis_index("col")
    partner_row = my_col // col_ratio
    tile_first = pair_lists[:, :, 0]
    tile_second = pair_lists[:, :, 1]
    packed = jnp.take(integrals, tile_second.reshape(-1), axis=2)
    packed = packed.reshape(occ_row, occ_col, row_devices, slot_count, square)
    received = lax.all_to_all(packed, "row", split_axis=2, concat_axis=0, tiled=True)
    received = received.reshape(occ_row * row_devices, occ_col, slot_count, square)
    piece = lax.all_gather(amplitudes, "col", axis=1, tiled=True)
    piece_count = piece.shape[1]
    left_tiles = piece.reshape(occ_row, piece_count, slot_count, tile_width, tile_width)
    right_tiles = received.reshape(piece_count, occ_col, slot_count, tile_width, tile_width)
    cycle_sum = jnp.einsum(
        "iksac,kjscb->ijsab", left_tiles, right_tiles, preferred_element_type=jnp.float32
    )
    my_count = lax.dynamic_index_in_dim(tile_counts, my_row, 0, keepdims=False)
    live_slots = (jnp.arange(slot_count, dtype=jnp.int32) < my_count).astype(jnp.float32)
    cycle_value = (cycle_sum * live_slots[None, None, :, None, None]).astype(jnp.bfloat16)
    cycle = cycle_value.reshape(occ_row, occ_col, slot_count, square)
    residual_strip = lax.all_gather(cycle, "row", axis=0, tiled=True)
    mirror_whole = lax.all_to_all(residual_strip, "col", split_axis=0, concat_axis=1, tiled=True)
    mirror_block = lax.dynamic_slice_in_dim(mirror_whole, my_row * occ_row, occ_row, 1)
    mirror_block = mirror_block.reshape(occ_col, occ_row, slot_count, tile_width, tile_width)
    mine_first = lax.dynamic_index_in_dim(tile_first, my_row, 0, keepdims=False)
    mine_second = lax.dynamic_index_in_dim(tile_second, my_row, 0, keepdims=False)
    their_first = lax.dynamic_index_in_dim(tile_first, partner_row, 0, keepdims=False)
    their_second = lax.dynamic_index_in_dim(tile_second, partner_row, 0, keepdims=False)
    pair_match = (
        (mine_first[:, None] == their_second[None, :])
        & (mine_second[:, None] == their_first[None, :])
    ).astype(jnp.bfloat16)
    crossed = jnp.einsum(
        "st,jitba->ijsab", pair_match, mirror_block, preferred_element_type=jnp.float32
    )
    own_part = cycle_value.astype(jnp.float32)
    symmetric = (own_part + crossed) * live_slots[None, None, :, None, None]
    return symmetric.reshape(occ_row, occ_col, slot_count, square)


def solution(mesh):
    return jax.shard_map(
        on_device,
        mesh=mesh,
        in_specs=(P("row", "col", None, None), P("row", "col", None, None), P(), P()),
        out_specs=P("row", "col", None, None),
        check_vma=False,
    )
```

profile of v0, /device:TPU:0, one launch (start us, length us, event | category | flops | bytes accessed | tf_op | source)
XLA Modules:
  0.0 288.4 jit_solution(7167490492308642510)
XLA Ops:
  6.5 0.0 copy-start
  6.5 0.0 all-gather.3.cloned.1.call-start
  6.5 2.8 copy.17
  9.3 0.0 all-gather.3.cloned.1.call-update
  9.3 0.8 fusion.29
  10.1 0.1 reshape_squeeze.6
  10.2 0.0 copy-done
  10.2 8.5 %gather_fusion = bf16[48,4,2,4096]{3,2,1,0:T(2,128)(2,1)} fusion(bf16[4,2,47,4096]{3,1,2,0:T(2,128)(2,1)S(1)} %copy-done, s32[1024]{0:T(1024)S(1)} %pad_clamp_fusion), kind=kCustom, calls=%fused_computation | custom fusion | bytes 6291648 | tf_op jit(solution)/shard_map/jit(_take)/gather | solution.py:20
  18.8 6.7 %broadcast_select_fusion = bf16[4,2,4,12,4096]{4,1,3,0,2:T(2,128)(2,1)} fusion(pred[4,12]{1,0:T(4,128)(4,1)S(1)} %compare_and_fusion, bf16[4,2,4,12,4096]{4,1,0,3,2:T(2,128)(2,1)} %bitcast.67), kind=kLoop, calls=%fused_computation.4 | loop fusion | flops 1572864 | bytes 6291504 | tf_op jit(solution)/shard_map/jit(_take)/select_n | solution.py:20
  25.4 0.0 copy-start.4
  25.4 6.4 %all-to-all-start = ((bf16[4,2,4,12,4096]{4,1,3,0,2:T(2,128)(2,1)}), bf16[4,2,4,12,4096]{4,1,3,0,2:T(2,128)(2,1)}, u32[]{:S(2)}, u32[]{:S(2)}) async-start(bf16[4,2,4,12,4096]{4,1,3,0,2:T(2,128)(2,1)} %broadcast_select_fusion), calls=%async_computation | async-start | bytes 6291456 | tf_op jit(solution)/shard_map/all_to_all | solution.py:22
  31.9 0.0 all-gather.5.cloned.1.call-start
  31.9 0.0 copy-done.4
  31.9 0.6 dynamic_slice.20
  32.5 0.6 compare_convert_fusion
  33.1 69.6 %all-to-all-done = bf16[4,2,4,12,4096]{4,1,3,0,2:T(2,128)(2,1)} async-done(((bf16[4,2,4,12,4096]{4,1,3,0,2:T(2,128)(2,1)}), bf16[4,2,4,12,4096]{4,1,3,0,2:T(2,128)(2,1)}, u32[]{:S(2)}, u32[]{:S(2)}) %all-to-all-start) | async-done | bytes 3145760 | tf_op jit(solution)/shard_map/all_to_all | solution.py:22
  102.7 11.1 %reshape_reshape.3 = bf16[16,2,12,64,64]{4,3,1,2,0:T(8,128)(2,1)} reshape(bf16[4,4,2,1,12,4096]{5,2,4,1,0,3:T(2,128)(2,1)} %bitcast.5) | data formatting | bytes 6291456 | tf_op jit(solution)/shard_map/reshape;reshape | solution.py:27
  113.8 0.0 all-gather.3.cloned.1.call-done
  113.8 9.4 %copy.18 = bf16[4,16,12,4096]{3,1,0,2:T(8,128)(2,1)} copy(bf16[4,16,12,4096]{3,0,2,1:T(4,128)(2,1)} %all-gather.3.cloned.1.call-done) | data formatting | bytes 12582912 | tf_op jit(solution)/shard_map/all_gather | solution.py:24
  123.2 17.9 %reshape.81 = bf16[4,16,12,64,64,1]{4,3,1,0,2,5:T(8,128)(2,1)} reshape(bf16[4,16,12,4096]{3,1,0,2:T(8,128)(2,1)} %copy.18) | data formatting | bytes 12582912 | tf_op jit(solution)/shard_map/reshape | solution.py:26
  141.1 11.1 %fusion.11 = bf16[4,2,12,64,64]{3,4,0,1,2:T(8,128)(2,1)S(1)} fusion(f32[12]{0:T(128)S(1)} %compare_convert_fusion, bf16[4,16,12,64,64,1]{4,3,1,0,2,5:T(8,128)(2,1)} %reshape.81, bf16[16,2,12,64,64]{4,3,1,2,0:T(8,128)(2,1)} %reshape_reshape.3), kind=kOutput, calls=%fused_computation.11 | convolution fusion | flops 806092800 | bytes 10223664 | tf_op jit(solution)/shard_map/iksac,kjscb->ijsab/dot_general | solution.py:28
  152.2 0.0 copy-start.2
  152.2 1.7 copy.20
  153.9 3.9 %reshape.69 = bf16[4,2,12,4096]{3,1,2,0:T(2,128)(2,1)} reshape(bf16[4,2,12,64,64]{4,3,1,2,0:T(8,128)(2,1)} %copy.20) | data formatting | bytes 1572864 | tf_op jit(solution)/shard_map/reshape | solution.py:34
  157.7 0.0 all-gather.5.cloned.1.call-update
  157.8 0.0 copy-done.2
  157.8 62.7 %all-gather.5.cloned.1.call-done = bf16[16,2,12,4096]{3,1,2,0:T(2,128)(2,1)} async-done(((bf16[4,2,12,4096]{3,1,2,0:T(2,128)(2,1)}), bf16[16,2,12,4096]{3,1,2,0:T(2,128)(2,1)}) %all-gather.5.cloned.1.call-update) | async-done | bytes 3145744 | tf_op jit(solution)/shard_map/all_gather | solution.py:35
  220.4 4.7 %all-to-all-start.1 = ((bf16[16,2,12,4096]{3,1,2,0:T(2,128)(2,1)}), bf16[16,2,12,4096]{3,1,2,0:T(2,128)(2,1)}, u32[]{:S(2)}, u32[]{:S(2)}) async-start(bf16[16,2,12,4096]{3,1,2,0:T(2,128)(2,1)} %all-gather.5.cloned.1.call-done), calls=%async_computation.1 | async-start | bytes 6291456 | tf_op jit(solution)/shard_map/all_to_all | solution.py:36
  225.2 37.6 %all-to-all-done.1 = bf16[16,2,12,4096]{3,1,2,0:T(2,128)(2,1)} async-done(((bf16[16,2,12,4096]{3,1,2,0:T(2,128)(2,1)}), bf16[16,2,12,4096]{3,1,2,0:T(2,128)(2,1)}, u32[]{:S(2)}, u32[]{:S(2)}) %all-to-all-start.1) | async-done | bytes 3145760 | tf_op jit(solution)/shard_map/all_to_all | solution.py:36
  262.8 5.1 %copy.21 = bf16[8,2,2,12,4096]{4,1,3,2,0:T(2,128)(2,1)S(1)} copy(bf16[8,2,2,12,4096]{4,2,3,1,0:T(2,128)(2,1)} %bitcast.12) | data formatting | bytes 6291456 | tf_op jit(solution)/shard_map/all_to_all | solution.py:36
  267.9 0.7 constant_dynamic-slice_fusion.4
  268.6 1.0 reshape.85
  269.6 0.0 copy-start.3
  269.6 1.1 fusion.5
  270.7 0.3 copy-done.3
  271.0 2.7 fusion.3
  273.7 0.0 copy-start.1
  273.7 3.7 %copy.25 = f32[4,2,12,64,64]{4,3,1,2,0:T(8,128)} copy(f32[4,2,12,64,64]{3,4,0,1,2:T(8,128)} %fusion.3) | data formatting | bytes 3145728 | tf_op jit(solution)/shard_map/mul | solution.py:51
  277.4 4.2 %reshape.71 = f32[4,2,12,4096]{3,1,2,0:T(2,128)} reshape(f32[4,2,12,64,64]{4,3,1,2,0:T(8,128)} %copy.25) | data formatting | bytes 3145728 | tf_op jit(solution)/shard_map/reshape | solution.py:52
  281.6 0.0 copy-done.1
  (4 shorter events, 0.0 us)
Async XLA Ops:
  6.5 3.7 %copy-start = (bf16[4,2,47,4096]{3,1,2,0:T(2,128)(2,1)S(1)}, bf16[4,2,47,4096]{3,1,2,0:T(2,128)(2,1)}, u32[]{:S(2)}) copy-start(bf16[4,2,47,4096]{3,1,2,0:T(2,128)(2,1)} %param.5) | copy-start | bytes 9240580
  6.5 107.3 %all-gather.3.cloned.1.call-start = ((), (), s32[]{:S(2)}) async-start(), calls=%async_computation.2 | async-start | bytes 7077888 | tf_op jit(solution)/shard_map/all_gather | solution.py:24
  25.4 6.4 %copy-start.4 = (s32[4]{0:T(128)S(1)}, s32[4]{0:T(128)}, u32[]{:S(2)}) copy-start(s32[4]{0:T(128)} %param.7) | copy-start | bytes 52
  25.4 77.3 %all-to-all-start = ((bf16[4,2,4,12,4096]{4,1,3,0,2:T(2,128)(2,1)}), bf16[4,2,4,12,4096]{4,1,3,0,2:T(2,128)(2,1)}, u32[]{:S(2)}, u32[]{:S(2)}) async-start(bf16[4,2,4,12,4096]{4,1,3,0,2:T(2,128)(2,1)} %broadcast_select_fusion), calls=%async_computation | async-start | bytes 6291456 | tf_op jit(solution)/shard_map/all_to_all | solution.py:22
  31.9 188.6 %all-gather.5.cloned.1.call-start = ((), (), s32[]{:S(2)}) async-start(), calls=%async_computation.3 | async-start | bytes 3932160 | tf_op jit(solution)/shard_map/all_gather | solution.py:35
  152.2 5.6 %copy-start.2 = (bf16[4,2,12,64,64]{3,4,0,1,2:T(8,128)(2,1)}, bf16[4,2,12,64,64]{3,4,0,1,2:T(8,128)(2,1)S(1)}, u32[]{:S(2)}) copy-start(bf16[4,2,12,64,64]{3,4,0,1,2:T(8,128)(2,1)S(1)} %fusion.11) | copy-start | bytes 2359300
  220.4 42.3 %all-to-all-start.1 = ((bf16[16,2,12,4096]{3,1,2,0:T(2,128)(2,1)}), bf16[16,2,12,4096]{3,1,2,0:T(2,128)(2,1)}, u32[]{:S(2)}, u32[]{:S(2)}) async-start(bf16[16,2,12,4096]{3,1,2,0:T(2,128)(2,1)} %all-gather.5.cloned.1.call-done), calls=%async_computation.1 | async-start | bytes 6291456 | tf_op jit(solution)/shard_map/all_to_all | solution.py:36
  269.6 1.4 copy-start.3
  273.7 7.9 %copy-start.1 = (bf16[4,2,47,4096]{3,1,2,0:T(2,128)(2,1)S(1)}, bf16[4,2,47,4096]{3,1,2,0:T(2,128)(2,1)}, u32[]{:S(2)}) copy-start(bf16[4,2,47,4096]{3,1,2,0:T(2,128)(2,1)} %param.5) | copy-start | bytes 9240580
Sparse Core Ops, SparseCore 0:
  9.5 48.1 all-gather.2
  157.9 62.5 all-gather.4
where the time goes:
time: 290 us; the launch traced here: 288 us
  waiting for transfers between devices  170 us (59%)
  local copies, waits for them, and re-layouts  71.7 us (25%)
  between operations  13.5 us (5%)
  matrix products  12.2 us (4%)
  starting transfers between devices  11.1 us (4%)
  other arithmetic  10 us (3%)
    all_to_all x1, waiting for transfers between devices, on_device(): lax.all_to_all(packed, 'row', split_axis=2, concat_axis=0, tiled=True)  69.6 us
    all_gather x1, waiting for transfers between devices, on_device(): residual_strip = lax.all_gather(cycle, 'row', axis=0, tiled=True)  62.7 us
    all_to_all x1, waiting for transfers between devices, on_device(): lax.all_to_all(residual_strip, 'col', split_axis=0, concat_axis=1, tiled=...  37.6 us
    reshape x1, local copies, waits for them, and re-layouts, on_device(): piece.reshape(occ_row, piece_count, slot_count, tile_width, tile_width)  17.9 us
    another operation x1, local copies, waits for them, and re-layouts, on_device(): received.reshape(piece_count, occ_col, slot_count, tile_width, tile_width)  11.1 us
    dot_general x1, matrix products, on_device(): jnp.einsum('iksac,kjscb->ijsab', left_tiles, right_tiles, preferred_eleme...  11.1 us
    all_gather x1, local copies, waits for them, and re-layouts, on_device(): piece = lax.all_gather(amplitudes, 'col', axis=1, tiled=True)  9.35 us
    gather x1, local copies, waits for them, and re-layouts, on_device(): packed = jnp.take(integrals, tile_second.reshape(-1), axis=2)  8.51 us
  transfers between devices with their start and end apart: 4, of which 3 were waited for; matrix products, arithmetic and copies ran while one was open for 10% of the time, Pallas kernels for 0%

commit v1 on v0

--- a/solution.py
+++ b/solution.py
@@ -19,7 +19,10 @@
     tile_second = pair_lists[:, :, 1]
     packed = jnp.take(integrals, tile_second.reshape(-1), axis=2)
     packed = packed.reshape(occ_row, occ_col, row_devices, slot_count, square)
-    received = lax.all_to_all(packed, "row", split_axis=2, concat_axis=0, tiled=True)
+    received = jnp.concatenate(
+        lax.all_to_all(jnp.stack(jnp.split(packed, lax.axis_size("row"), axis=2)), "row", 0, 0),
+        axis=0,
+    )
     received = received.reshape(occ_row * row_devices, occ_col, slot_count, square)
     piece = lax.all_gather(amplitudes, "col", axis=1, tiled=True)
     piece_count = piece.shape[1]

time: 290 us -> 301 us (1.038)
  local copies, waits for them, and re-layouts: 71.7 us -> 79.8 us
    another operation x0 -> x1, other arithmetic: none -> 6.62 us  [on_device(): jnp.stack(jnp.split(packed, lax.axis_size('row'), axis=2))]
    gather x1 -> x2, local copies, waits for them, and re-layouts: 8.51 us -> 13.8 us  [on_device(): packed = jnp.take(integrals, tile_second.reshape(-1), axis=2)]
    select_n x2, other arithmetic: 6.69 us -> 2.91 us  [on_device(): packed = jnp.take(integrals, tile_second.reshape(-1), axis=2)]
  transfers between devices with their start and end apart: 4 -> 4, of which waited for: 3 -> 3; matrix products, arithmetic and copies ran while one was open for 10% -> 13% of each run, Pallas kernels for 0% -> 0%
where the time goes in v1:
time: 301 us; the launch traced here: 299 us
  waiting for transfers between devices  170 us (56%)
  local copies, waits for them, and re-layouts  79.8 us (27%)
  between operations  13.5 us (4%)
  other arithmetic  12.9 us (4%)
  matrix products  12.2 us (4%)
  starting transfers between devices  11.1 us (4%)
    all_to_all x1, waiting for transfers between devices, on_device(): lax.all_to_all(jnp.stack(jnp.split(packed, lax.axis_size('row'), axis=2))...  69.5 us
    all_gather x1, waiting for transfers between devices, on_device(): residual_strip = lax.all_gather(cycle, 'row', axis=0, tiled=True)  62.7 us
    all_to_all x1, waiting for transfers between devices, on_device(): lax.all_to_all(residual_strip, 'col', split_axis=0, concat_axis=1, tiled=...  37.6 us
    reshape x1, local copies, waits for them, and re-layouts, on_device(): piece.reshape(occ_row, piece_count, slot_count, tile_width, tile_width)  17.9 us
    gather x2, local copies, waits for them, and re-layouts, on_device(): packed = jnp.take(integrals, tile_second.reshape(-1), axis=2)  13.8 us
    dot_general x1, matrix products, on_device(): jnp.einsum('iksac,kjscb->ijsab', left_tiles, right_tiles, preferred_eleme...  11.1 us
    another operation x1, local copies, waits for them, and re-layouts, on_device(): received.reshape(piece_count, occ_col, slot_count, tile_width, tile_width)  11.1 us
    all_gather x1, local copies, waits for them, and re-layouts, on_device(): piece = lax.all_gather(amplitudes, 'col', axis=1, tiled=True)  9.35 us
  transfers between devices with their start and end apart: 4, of which 3 were waited for; matrix products, arithmetic and copies ran while one was open for 13% of the time, Pallas kernels for 0%

profile of v1, /device:TPU:0, one launch (start us, length us, event | category | flops | bytes accessed | tf_op | source)
XLA Modules:
  0.0 299.3 jit_solution(5662175506649471996)
XLA Ops:
  6.5 0.0 copy-start
  6.5 0.0 all-gather.3.cloned.1.call-start
  6.5 2.8 copy.32
  9.3 0.0 all-gather.3.cloned.1.call-update
  9.3 0.8 fusion.29
  10.1 0.1 reshape_squeeze.6
  10.2 0.0 copy-done
  10.2 8.5 %gather_fusion = bf16[48,4,2,4096]{3,2,1,0:T(2,128)(2,1)} fusion(bf16[4,2,47,4096]{3,1,2,0:T(2,128)(2,1)S(1)} %copy-done, s32[1024]{0:T(1024)S(1)} %pad_clamp_fusion), kind=kCustom, calls=%fused_computation | custom fusion | bytes 6291648 | tf_op jit(solution)/shard_map/jit(_take)/gather | solution.py:20
  18.7 5.2 %copy.28 = bf16[4,2,48,4096]{3,1,2,0:T(2,128)(2,1)S(1)} copy(bf16[4,2,48,4096]{3,1,0,2:T(2,128)(2,1)} %bitcast.78) | data formatting | bytes 6291456 | tf_op jit(solution)/shard_map/jit(_take)/gather | solution.py:20
  24.0 2.9 broadcast_select_fusion
  26.9 2.8 slice_bitcast_fusion.3
  29.8 6.6 %pad_maximum_fusion = bf16[4,4,2,1,12,4096]{5,2,4,1,3,0:T(2,128)(2,1)} fusion(bf16[1,4,2,1,12,4096]{5,2,4,1,3,0:T(2,128)(2,1)S(1)} %get-tuple-element.7, bf16[1,4,2,1,12,4096]{5,2,4,1,3,0:T(2,128)(2,1)S(1)} %get-tuple-element.8, bf16[1,4,2,1,12,4096]{5,2,4,1,3,0:T(2,128)(2,1)S(1)} %get-tuple-element.6, bf16[1,4,2,1,12,4096]{5,2,4,1,3,0:T(2,128)(2,1)S(1)} %get-tuple-element.5), kind=kLoop, calls=%fused_computation.5 | loop fusion | flops 4718592 | bytes 6291456 | tf_op jit(solution)/shard_map/stack | solution.py:23
  36.4 0.0 copy-start.4
  36.4 6.4 %all-to-all-start = ((bf16[4,4,2,1,12,4096]{5,2,4,1,3,0:T(2,128)(2,1)}), bf16[4,4,2,1,12,4096]{5,2,4,1,3,0:T(2,128)(2,1)}, u32[]{:S(2)}, u32[]{:S(2)}) async-start(bf16[4,4,2,1,12,4096]{5,2,4,1,3,0:T(2,128)(2,1)} %pad_maximum_fusion), calls=%async_computation | async-start | bytes 6291456 | tf_op jit(solution)/shard_map/all_to_all | solution.py:23
  42.8 0.0 all-gather.5.cloned.1.call-start
  42.8 0.0 copy-done.4
  42.8 0.7 dynamic_slice.20
  43.5 0.7 compare_convert_fusion
  44.2 69.5 %all-to-all-done = bf16[4,4,2,1,12,4096]{5,2,4,1,3,0:T(2,128)(2,1)} async-done(((bf16[4,4,2,1,12,4096]{5,2,4,1,3,0:T(2,128)(2,1)}), bf16[4,4,2,1,12,4096]{5,2,4,1,3,0:T(2,128)(2,1)}, u32[]{:S(2)}, u32[]{:S(2)}) %all-to-all-start) | async-done | bytes 3145760 | tf_op jit(solution)/shard_map/all_to_all | solution.py:23
  113.7 11.1 %reshape_reshape_reshape.3 = bf16[16,2,12,64,64]{4,3,1,2,0:T(8,128)(2,1)} reshape(bf16[4,4,2,1,12,4096]{5,2,4,1,3,0:T(2,128)(2,1)} %all-to-all-done) | data formatting | bytes 6291456 | tf_op jit(solution)/shard_map/reshape;reshape;reshape | solution.py:30
  124.7 0.0 all-gather.3.cloned.1.call-done
  124.7 9.3 %copy.33 = bf16[4,16,12,4096]{3,1,0,2:T(8,128)(2,1)} copy(bf16[4,16,12,4096]{3,0,2,1:T(4,128)(2,1)} %all-gather.3.cloned.1.call-done) | data formatting | bytes 12582912 | tf_op jit(solution)/shard_map/all_gather | solution.py:27
  134.1 17.9 %reshape.80 = bf16[4,16,12,64,64,1]{4,3,1,0,2,5:T(8,128)(2,1)} reshape(bf16[4,16,12,4096]{3,1,0,2:T(8,128)(2,1)} %copy.33) | data formatting | bytes 12582912 | tf_op jit(solution)/shard_map/reshape | solution.py:29
  152.0 11.1 %fusion.11 = bf16[4,2,12,64,64]{3,4,0,1,2:T(8,128)(2,1)S(1)} fusion(f32[12]{0:T(128)S(1)} %compare_convert_fusion, bf16[4,16,12,64,64,1]{4,3,1,0,2,5:T(8,128)(2,1)} %reshape.80, bf16[16,2,12,64,64]{4,3,1,2,0:T(8,128)(2,1)} %reshape_reshape_reshape.3), kind=kOutput, calls=%fused_computation.12 | convolution fusion | flops 806092800 | bytes 10223664 | tf_op jit(solution)/shard_map/iksac,kjscb->ijsab/dot_general | solution.py:31
  163.1 0.0 copy-start.2
  163.1 1.7 copy.35
  164.8 3.8 %reshape.68 = bf16[4,2,12,4096]{3,1,2,0:T(2,128)(2,1)} reshape(bf16[4,2,12,64,64]{4,3,1,2,0:T(8,128)(2,1)} %copy.35) | data formatting | bytes 1572864 | tf_op jit(solution)/shard_map/reshape | solution.py:37
  168.6 0.0 all-gather.5.cloned.1.call-update
  168.6 0.0 copy-done.2
  168.7 62.7 %all-gather.5.cloned.1.call-done = bf16[16,2,12,4096]{3,1,2,0:T(2,128)(2,1)} async-done(((bf16[4,2,12,4096]{3,1,2,0:T(2,128)(2,1)}), bf16[16,2,12,4096]{3,1,2,0:T(2,128)(2,1)}) %all-gather.5.cloned.1.call-update) | async-done | bytes 3145744 | tf_op jit(solution)/shard_map/all_gather | solution.py:38
  231.3 4.7 %all-to-all-start.1 = ((bf16[16,2,12,4096]{3,1,2,0:T(2,128)(2,1)}), bf16[16,2,12,4096]{3,1,2,0:T(2,128)(2,1)}, u32[]{:S(2)}, u32[]{:S(2)}) async-start(bf16[16,2,12,4096]{3,1,2,0:T(2,128)(2,1)} %all-gather.5.cloned.1.call-done), calls=%async_computation.1 | async-start | bytes 6291456 | tf_op jit(solution)/shard_map/all_to_all | solution.py:39
  236.0 37.6 %all-to-all-done.1 = bf16[16,2,12,4096]{3,1,2,0:T(2,128)(2,1)} async-done(((bf16[16,2,12,4096]{3,1,2,0:T(2,128)(2,1)}), bf16[16,2,12,4096]{3,1,2,0:T(2,128)(2,1)}, u32[]{:S(2)}, u32[]{:S(2)}) %all-to-all-start.1) | async-done | bytes 3145760 | tf_op jit(solution)/shard_map/all_to_all | solution.py:39
  273.6 5.1 %copy.36 = bf16[8,2,2,12,4096]{4,1,3,2,0:T(2,128)(2,1)S(1)} copy(bf16[8,2,2,12,4096]{4,2,3,1,0:T(2,128)(2,1)} %bitcast.14) | data formatting | bytes 6291456 | tf_op jit(solution)/shard_map/all_to_all | solution.py:39
  278.8 0.7 constant_dynamic-slice_fusion.4
  279.4 1.0 reshape.84
  280.5 0.0 copy-start.3
  280.5 1.1 fusion.5
  281.6 0.3 copy-done.3
  281.9 2.7 fusion.3
  284.6 0.0 copy-start.1
  284.6 3.7 %copy.40 = f32[4,2,12,64,64]{4,3,1,2,0:T(8,128)} copy(f32[4,2,12,64,64]{3,4,0,1,2:T(8,128)} %fusion.3) | data formatting | bytes 3145728 | tf_op jit(solution)/shard_map/mul | solution.py:54
  288.3 4.2 %reshape.70 = f32[4,2,12,4096]{3,1,2,0:T(2,128)} reshape(f32[4,2,12,64,64]{4,3,1,2,0:T(8,128)} %copy.40) | data formatting | bytes 3145728 | tf_op jit(solution)/shard_map/reshape | solution.py:55
  292.5 0.0 copy-done.1
  (4 shorter events, 0.0 us)
Async XLA Ops:
  6.5 3.7 %copy-start = (bf16[4,2,47,4096]{3,1,2,0:T(2,128)(2,1)S(1)}, bf16[4,2,47,4096]{3,1,2,0:T(2,128)(2,1)}, u32[]{:S(2)}) copy-start(bf16[4,2,47,4096]{3,1,2,0:T(2,128)(2,1)} %param.5) | copy-start | bytes 9240580
  6.5 118.2 %all-gather.3.cloned.1.call-start = ((), (), s32[]{:S(2)}) async-start(), calls=%async_computation.2 | async-start | bytes 7077888 | tf_op jit(solution)/shard_map/all_gather | solution.py:27
  36.4 6.4 %copy-start.4 = (s32[4]{0:T(128)S(1)}, s32[4]{0:T(128)}, u32[]{:S(2)}) copy-start(s32[4]{0:T(128)} %param.7) | copy-start | bytes 52
  36.4 77.3 %all-to-all-start = ((bf16[4,4,2,1,12,4096]{5,2,4,1,3,0:T(2,128)(2,1)}), bf16[4,4,2,1,12,4096]{5,2,4,1,3,0:T(2,128)(2,1)}, u32[]{:S(2)}, u32[]{:S(2)}) async-start(bf16[4,4,2,1,12,4096]{5,2,4,1,3,0:T(2,128)(2,1)} %pad_maximum_fusion), calls=%async_computation | async-start | bytes 6291456 | tf_op jit(solution)/shard_map/all_to_all | solution.py:23
  42.8 188.5 %all-gather.5.cloned.1.call-start = ((), (), s32[]{:S(2)}) async-start(), calls=%async_computation.3 | async-start | bytes 3932160 | tf_op jit(solution)/shard_map/all_gather | solution.py:38
  163.1 5.5 %copy-start.2 = (bf16[4,2,12,64,64]{3,4,0,1,2:T(8,128)(2,1)}, bf16[4,2,12,64,64]{3,4,0,1,2:T(8,128)(2,1)S(1)}, u32[]{:S(2)}) copy-start(bf16[4,2,12,64,64]{3,4,0,1,2:T(8,128)(2,1)S(1)} %fusion.11) | copy-start | bytes 2359300
  231.3 42.3 %all-to-all-start.1 = ((bf16[16,2,12,4096]{3,1,2,0:T(2,128)(2,1)}), bf16[16,2,12,4096]{3,1,2,0:T(2,128)(2,1)}, u32[]{:S(2)}, u32[]{:S(2)}) async-start(bf16[16,2,12,4096]{3,1,2,0:T(2,128)(2,1)} %all-gather.5.cloned.1.call-done), calls=%async_computation.1 | async-start | bytes 6291456 | tf_op jit(solution)/shard_map/all_to_all | solution.py:39
  280.5 1.4 copy-start.3
  284.6 7.9 %copy-start.1 = (bf16[4,2,47,4096]{3,1,2,0:T(2,128)(2,1)S(1)}, bf16[4,2,47,4096]{3,1,2,0:T(2,128)(2,1)}, u32[]{:S(2)}) copy-start(bf16[4,2,47,4096]{3,1,2,0:T(2,128)(2,1)} %param.5) | copy-start | bytes 9240580
Sparse Core Ops, SparseCore 0:
  9.5 48.1 all-gather.2
  168.8 62.4 all-gather.4
